TPU v7x, 32 devices: a whole 2x2x4 slice. The times are simulated.
32 devices in a mesh: groups: 2 (over x), tensor: 16 (over z, y, core).
Axes of the slice: x: 2, y: 2, z: 4, core: 2. Of those that a mesh axis runs over, the one named last changes fastest.
Arguments:
- tokens: bfloat16 [1024, 8192], P('groups', 'tensor'), parts along dimension 0, may hold values from -6 to 6
- norm_gain: float32 [8192], P('tensor'), may hold values from 0.1 to 1.9
- w_in: bfloat16 [8192, 3, 8192], P(None, None, 'tensor'), may hold values from -0.0625 to 0.0625
- w_short: float32 [3, 3, 8192], P(None, None, 'tensor'), may hold values from -3 to 3
- filters: bfloat16 [512, 128], P('tensor'), may hold values from -0.5 to 0.5
- skip: float32 [8192], P('tensor'), may hold values from -4 to 4
- w_out: bfloat16 [8192, 8192], P('tensor'), may hold values from -0.0625 to 0.0625
Outputs:
- mixed: bfloat16 [1024, 8192], P('groups', 'tensor'), parts along dimension 0
There are 2 independent parts, one for each index of `groups`. A program takes and returns all parts, laid end to end along the dimension named above; an argument that names none is the same for every part. Nothing has to cross between parts.
All inputs are finite; a program needn't handle non-finite values.
Results may differ from a plain program's by a relative error of at most 0.0085.
Values may be sent and summed in bfloat16 or wider, within the bound.
A program may use at most 192 MiB of HBM per device.

v0:
```python
import jax
import jax.numpy as jnp
from jax import lax
from jax.sharding import PartitionSpec as P

D = 8192


def shifted(field, lag):
    pads = ((lag, 0),) + ((0, 0),) * (field.ndim - 1)
    return jnp.pad(field, pads)[: field.shape[0]]


def lag_matrix(filters, rows):
    count, taps = filters.shape
    length = taps + rows
    line = jnp.concatenate([filters, jnp.zeros((count, rows), filters.dtype)], axis=1)
    tiled = jnp.tile(line, (1, rows))[:, : rows * (length - 1)]
    return tiled.reshape(count, rows, length - 1)[:, :, :rows]


def on_device(tokens, norm_gain, w_in, w_short, filters, skip, w_out):
    wide = tokens.astype(jnp.float32)
    squares = lax.psum(jnp.sum(wide * wide, axis=1, keepdims=True), "tensor")
    factor = lax.rsqrt(squares / D + 1e-05)
    normed = (wide * factor * norm_gain[None, :]).astype(jnp.bfloat16)
    width = w_in.shape[0]
    local = w_in.shape[2]
    rows = tokens.shape[0]
    w_flat = w_in.reshape(width, 3 * local)
    chosen = w_flat
    proj = jnp.dot(
        lax.all_gather(normed, "tensor", axis=1, tiled=True),
        chosen,
        preferred_element_type=jnp.float32,
    )
    proj = proj.reshape(rows, 3, local)
    short = w_short[0][None] * proj
    for lag in range(1, w_short.shape[0]):
        short = short + w_short[lag][None] * shifted(proj, lag)
    gated = (short[:, 1] * short[:, 2]).astype(jnp.bfloat16)
    count = filters.shape[0]
    lagged = lag_matrix(filters, rows)
    grouped = gated.reshape(rows, count, local // count)
    conv = jnp.einsum("fst,sfg->tfg", lagged, grouped, preferred_element_type=jnp.float32)
    conv = conv.reshape(rows, local)
    hidden = ((conv + skip[None, :] * gated.astype(jnp.float32)) * short[:, 0]).astype(jnp.bfloat16)
    w_cols = lax.all_to_all(w_out, "tensor", split_axis=1, concat_axis=0, tiled=True)
    chosen = w_cols
    summed = jnp.dot(
        lax.all_gather(hidden, "tensor", axis=1, tiled=True),
        chosen,
        preferred_element_type=jnp.float32,
    )
    return (wide + summed).astype(jnp.bfloat16)


def solution(mesh):
    return jax.shard_map(
        on_device,
        mesh=mesh,
        in_specs=(
            P("groups", "tensor"),
            P("tensor"),
            P(None, None, "tensor"),
            P(None, None, "tensor"),
            P("tensor", None),
            P("tensor"),
            P("tensor", None),
        ),
        out_specs=P("groups", "tensor"),
        check_vma=False,
    )
```

profile of v0, /device:TPU:0, one launch (start us, length us, event | category | flops | bytes accessed | tf_op | source)
XLA Modules:
  0.0 382.3 jit_solution(3870038537014596827)
XLA Ops:
  6.5 1.2 fusion.10
  7.8 35.0 %psum.7 = f32[512,1]{0,1:T(1,128)S(1)} all-reduce(f32[512,1]{0,1:T(1,128)S(1)} %bitcast.46), channel_id=1, replica_groups=mesh['groups'=2,'tensor'=16] {'tensor'}, use_global_device_ids=true, to_apply=%region_1.0 | all-reduce | flops 512 | bytes 4096 | tf_op jit(solution)/shard_map/psum | solution.py:24
  42.7 2.0 fusion.12
  44.7 0.0 all-gather.3.cloned.1.call-update
  44.8 12.1 %copy.16 = bf16[512,8192]{0,1:T(8,128)(2,1)} copy(bf16[512,8192]{1,0:T(8,128)(2,1)} %param.13) | data formatting | bytes 16777216 | tf_op args[6]
  56.8 4.8 %all-to-all-start = ((bf16[512,16,512]{0,2,1:T(8,128)(2,1)}), bf16[512,16,512]{0,2,1:T(8,128)(2,1)}, u32[]{:S(2)}, u32[]{:S(2)}) async-start(bf16[512,16,512]{0,2,1:T(8,128)(2,1)} %bitcast.41), calls=%async_computation | async-start | bytes 16777216 | tf_op jit(solution)/shard_map/all_to_all | solution.py:48
  61.6 0.0 all-gather.5.cloned.1.call-start
  61.7 33.5 %copy.13 = bf16[8192,3,512]{0,2,1:T(8,128)(2,1)} copy(bf16[8192,3,512]{2,0,1:T(8,128)(2,1)} %param.9) | data formatting | bytes 50331648 | tf_op args[2]
  95.1 2.9 tile.4
  98.0 67.1 %copy.18 = bf16[4,8,512,640]{3,1,2,0:T(8,128)(2,1)S(1)} copy(bf16[4,8,512,640]{3,2,1,0:T(8,128)(2,1)S(1)} %bitcast.39) | data formatting | bytes 41943040
  165.1 8.1 %slice.42 = bf16[32,327168]{1,0:T(8,128)(2,1)} slice(bf16[32,327680]{1,0:T(8,128)(2,1)S(1)} %bitcast.40), slice={[0:32], [0:327168]} | slice | bytes 41877504 | tf_op jit(solution)/shard_map/slice | solution.py:18
  173.2 69.0 %reshape.30 = bf16[32,512,639]{2,1,0:T(8,128)(2,1)} reshape(bf16[32,327168]{1,0:T(8,128)(2,1)} %slice.42) | data formatting | bytes 41877504 | tf_op jit(solution)/shard_map/reshape | solution.py:19
  242.3 0.0 all-gather.3.cloned.1.call-done
  242.3 19.6 %fusion = f32[512,3,512]{2,0,1:T(8,128)S(1)} fusion(bf16[8192,3,512]{0,2,1:T(8,128)(2,1)} %copy.13, bf16[512,8192]{1,0:T(8,128)(2,1)} %all-gather.3.cloned.1.call-done), kind=kOutput, calls=%fused_computation | convolution fusion | flops 12884901888 | bytes 36700160 | tf_op jit(solution)/shard_map/dot_general | solution.py:32
  261.9 0.9 fusion.7
  262.8 0.9 fusion.15
  263.8 2.1 copy.14
  265.9 9.2 %fusion.2 = f32[32,16,512]{2,1,0:T(8,128)} fusion(bf16[512,32,16]{0,2,1:T(8,128)(2,1)} %bitcast.44, bf16[32,512,639]{2,1,0:T(8,128)(2,1)} %reshape.30), kind=kOutput, calls=%fused_computation.2 | convolution fusion | flops 268435456 | bytes 18350080 | tf_op jit(solution)/shard_map/fst,sfg->tfg/dot_general | solution.py:45
  275.1 2.6 copy.15
  277.7 2.5 fusion.14
  280.2 0.0 all-gather.5.cloned.1.call-update
  280.2 12.4 %copy.17 = bf16[16,512,512]{2,1,0:T(8,128)(2,1)} copy(bf16[16,512,512]{1,2,0:T(8,128)(2,1)} %bitcast.15) | data formatting | bytes 16777216 | tf_op jit(solution)/shard_map/all_to_all | solution.py:48
  292.6 71.8 %all-gather.5.cloned.1.call-done = bf16[512,8192]{1,0:T(8,128)(2,1)} async-done(((bf16[512,512]{1,0:T(8,128)(2,1)}), bf16[512,8192]{1,0:T(8,128)(2,1)}) %all-gather.5.cloned.1.call-update) | async-done | bytes 8388624 | tf_op jit(solution)/shard_map/all_gather | solution.py:51
  364.4 11.0 %fusion.9 = bf16[512,512]{1,0:T(8,128)(2,1)} fusion(bf16[512,8192]{1,0:T(8,128)(2,1)} %all-gather.5.cloned.1.call-done, bf16[8192,512]{1,0:T(8,128)(2,1)} %bitcast.43, bf16[512,512]{1,0:T(8,128)(2,1)S(1)} %copy-done), kind=kOutput, calls=%fused_computation.14 | convolution fusion | flops 4295753728 | bytes 17825792 | tf_op jit(solution)/shard_map/dot_general | solution.py:50
  (13 shorter events, 0.0 us)
Async XLA Ops:
  6.5 235.7 %all-gather.3.cloned.1.call-start = ((), (), s32[]{:S(2)}) async-start(), calls=%async_computation.1 | async-start | bytes 8912896 | tf_op jit(solution)/shard_map/all_gather | solution.py:33
  56.8 223.4 %all-to-all-start = ((bf16[512,16,512]{0,2,1:T(8,128)(2,1)}), bf16[512,16,512]{0,2,1:T(8,128)(2,1)}, u32[]{:S(2)}, u32[]{:S(2)}) async-start(bf16[512,16,512]{0,2,1:T(8,128)(2,1)} %bitcast.41), calls=%async_computation | async-start | bytes 16777216 | tf_op jit(solution)/shard_map/all_to_all | solution.py:48
  61.6 33.5 %copy-start.2 = (bf16[32,128]{1,0:T(8,128)(2,1)S(1)}, bf16[32,128]{1,0:T(8,128)(2,1)}, u32[]{:S(2)}) copy-start(bf16[32,128]{1,0:T(8,128)(2,1)} %param.11) | copy-start | bytes 24580
  61.6 302.8 %all-gather.5.cloned.1.call-start = ((), (), s32[]{:S(2)}) async-start(), calls=%async_computation.2 | async-start | bytes 8912896 | tf_op jit(solution)/shard_map/all_gather | solution.py:51
  173.2 69.0 %copy-start.1 = (f32[3,3,512]{2,1,0:T(4,128)S(1)}, f32[3,3,512]{2,1,0:T(4,128)}, u32[]{:S(2)}) copy-start(f32[3,3,512]{2,1,0:T(4,128)} %param.10) | copy-start | bytes 55300
  265.9 11.8 %copy-start.3 = (f32[512]{0:T(512)S(1)}, f32[512]{0:T(512)}, u32[]{:S(2)}) copy-start(f32[512]{0:T(512)} %param.12) | copy-start | bytes 6148
  280.2 84.2 %copy-start = (bf16[512,512]{1,0:T(8,128)(2,1)S(1)}, bf16[512,512]{1,0:T(8,128)(2,1)}, u32[]{:S(2)}) copy-start(bf16[512,512]{1,0:T(8,128)(2,1)} %param.7) | copy-start | bytes 1572868
Sparse Core Ops, SparseCore 0:
  44.9 189.7 all-gather.2
  280.3 84.0 all-gather.4
where the time goes:
time: 384 us; the launch traced here: 382 us
  local copies, waits for them, and re-layouts  210 us (55%)
  waiting for transfers between devices  71.8 us (19%)
  matrix products  39.9 us (10%)
  blocking collectives  35 us (9%)
  between operations  13.5 us (4%)
  other arithmetic  7.65 us (2%)
  starting transfers between devices  4.8 us (1%)
    unnamed x11, local copies, waits for them, and re-layouts  113 us
    all_gather x1, waiting for transfers between devices, on_device(): lax.all_gather(hidden, 'tensor', axis=1, tiled=True)  71.8 us
    reshape x1, local copies, waits for them, and re-layouts, lag_matrix(): return tiled.reshape(count, rows, length - 1)[:, :, :rows]  69 us
    psum x1, blocking collectives, on_device(): squares = lax.psum(jnp.sum(wide * wide, axis=1, keepdims=True), 'tensor')  35 us
    dot_general x1, matrix products, on_device(): jnp.dot(lax.all_gather(normed, 'tensor', axis=1, tiled=True), chosen, pre...  19.6 us
    all_to_all x1, local copies, waits for them, and re-layouts, on_device(): lax.all_to_all(w_out, 'tensor', split_axis=1, concat_axis=0, tiled=True)  12.4 us
    dot_general x1, matrix products, on_device(): jnp.dot(lax.all_gather(hidden, 'tensor', axis=1, tiled=True), chosen, pre...  11 us
    dot_general x1, matrix products, on_device(): jnp.einsum('fst,sfg->tfg', lagged, grouped, preferred_element_type=jnp.fl...  9.22 us
  transfers between devices with their start and end apart: 3, of which 1 were waited for; matrix products, arithmetic and copies ran while one was open for 64% of the time, Pallas kernels for 0%

commit v1 on v0

--- a/solution.py
+++ b/solution.py
@@ -4,6 +4,13 @@
 from jax.sharding import PartitionSpec as P
 
 D = 8192
+
+
+def post_set_up(z_in):
+    return jnp.concatenate(
+        lax.all_to_all(jnp.stack(jnp.split(z_in, lax.axis_size("tensor"), axis=1)), "tensor", 0, 0),
+        axis=0,
+    )
 
 
 def shifted(field, lag):
@@ -45,7 +52,7 @@
     conv = jnp.einsum("fst,sfg->tfg", lagged, grouped, preferred_element_type=jnp.float32)
     conv = conv.reshape(rows, local)
     hidden = ((conv + skip[None, :] * gated.astype(jnp.float32)) * short[:, 0]).astype(jnp.bfloat16)
-    w_cols = lax.all_to_all(w_out, "tensor", split_axis=1, concat_axis=0, tiled=True)
+    w_cols = post_set_up(w_out)
     chosen = w_cols
     summed = jnp.dot(
         lax.all_gather(hidden, "tensor", axis=1, tiled=True),

time: 384 us -> 398 us (1.036)
  waiting for transfers between devices: 71.8 us -> 79 us
  local copies, waits for them, and re-layouts: 210 us -> 215 us
    unnamed x11 -> x23, local copies, waits for them, and re-layouts: 113 us -> 129 us
    all_to_all x1 -> x0, local copies, waits for them, and re-layouts: 12.4 us -> none  [on_device(): lax.all_to_all(w_out, 'tensor', split_axis=1, concat_axis=0, tiled=True)]
    all_gather x1, waiting for transfers between devices: 71.8 us -> 78.9 us  [on_device(): lax.all_gather(hidden, 'tensor', axis=1, tiled=True)]
  transfers between devices with their start and end apart: 3 -> 3, of which waited for: 1 -> 1; matrix products, arithmetic and copies ran while one was open for 64% -> 63% of each run, Pallas kernels for 0% -> 0%
where the time goes in v1:
time: 398 us; the launch traced here: 395 us
  local copies, waits for them, and re-layouts  215 us (54%)
  waiting for transfers between devices  79 us (20%)
  matrix products  39.9 us (10%)
  blocking collectives  35 us (9%)
  between operations  13.5 us (3%)
  other arithmetic  7.65 us (2%)
  starting transfers between devices  4.96 us (1%)
    unnamed x23, local copies, waits for them, and re-layouts  129 us
    all_gather x1, waiting for transfers between devices, on_device(): lax.all_gather(hidden, 'tensor', axis=1, tiled=True)  78.9 us
    reshape x1, local copies, waits for them, and re-layouts, lag_matrix(): return tiled.reshape(count, rows, length - 1)[:, :, :rows]  69 us
    psum x1, blocking collectives, on_device(): squares = lax.psum(jnp.sum(wide * wide, axis=1, keepdims=True), 'tensor')  35 us
    dot_general x1, matrix products, on_device(): jnp.dot(lax.all_gather(normed, 'tensor', axis=1, tiled=True), chosen, pre...  19.6 us
    dot_general x1, matrix products, on_device(): jnp.dot(lax.all_gather(hidden, 'tensor', axis=1, tiled=True), chosen, pre...  11.1 us
    dot_general x1, matrix products, on_device(): jnp.einsum('fst,sfg->tfg', lagged, grouped, preferred_element_type=jnp.fl...  9.23 us
    slice x1, local copies, waits for them, and re-layouts, lag_matrix(): tiled = jnp.tile(line, (1, rows))[:, :rows * (length - 1)]  8.08 us
  transfers between devices with their start and end apart: 3, of which 1 were waited for; matrix products, arithmetic and copies ran while one was open for 63% of the time, Pallas kernels for 0%

profile of v1, /device:TPU:0, one launch (start us, length us, event | category | flops | bytes accessed | tf_op | source)
XLA Modules:
  0.0 395.4 jit_solution(1132656147243223446)
XLA Ops:
  7.8 35.0 %psum.7 = f32[512,1]{0,1:T(1,128)S(1)} all-reduce(f32[512,1]{0,1:T(1,128)S(1)} %bitcast.74), channel_id=1, replica_groups=mesh['groups'=2,'tensor'=16] {'tensor'}, use_global_device_ids=true, to_apply=%region_1.0 | all-reduce | flops 512 | bytes 4096 | tf_op jit(solution)/shard_map/psum | solution.py:31
  42.7 2.0 fusion.12
  44.8 1.9 bitcast_dynamic-update-slice_fusion.15
  46.7 1.9 bitcast_dynamic-update-slice_fusion.14
  48.5 1.9 bitcast_dynamic-update-slice_fusion.13
  50.5 1.9 bitcast_dynamic-update-slice_fusion.12
  52.4 1.9 bitcast_dynamic-update-slice_fusion.11
  54.3 1.9 bitcast_dynamic-update-slice_fusion.10
  63.6 1.9 bitcast_dynamic-update-slice_fusion.5
  69.2 1.9 bitcast_dynamic-update-slice_fusion.2
  73.0 1.9 bitcast_dynamic-update-slice_fusion
  74.9 4.9 %all-to-all-start = ((bf16[16,512,512]{2,1,0:T(8,128)(2,1)}), bf16[16,512,512]{2,1,0:T(8,128)(2,1)}, u32[]{:S(2)}, u32[]{:S(2)}) async-start(bf16[16,512,512]{2,1,0:T(8,128)(2,1)} %bitcast_dynamic-update-slice_fusion), calls=%async_computation | async-start | bytes 16777216 | tf_op jit(solution)/shard_map/all_to_all | solution.py:11
  79.9 33.6 %copy.10 = bf16[8192,3,512]{0,2,1:T(8,128)(2,1)} copy(bf16[8192,3,512]{2,0,1:T(8,128)(2,1)} %param.9) | data formatting | bytes 50331648 | tf_op args[2]
  113.5 2.9 tile.4
  116.4 67.1 %copy.13 = bf16[4,8,512,640]{3,1,2,0:T(8,128)(2,1)S(1)} copy(bf16[4,8,512,640]{3,2,1,0:T(8,128)(2,1)S(1)} %bitcast.69) | data formatting | bytes 41943040
  183.5 8.1 %slice.42 = bf16[32,327168]{1,0:T(8,128)(2,1)} slice(bf16[32,327680]{1,0:T(8,128)(2,1)S(1)} %bitcast.70), slice={[0:32], [0:327168]} | slice | bytes 41877504 | tf_op jit(solution)/shard_map/slice | solution.py:25
  191.6 69.0 %reshape.30 = bf16[32,512,639]{2,1,0:T(8,128)(2,1)} reshape(bf16[32,327168]{1,0:T(8,128)(2,1)} %slice.42) | data formatting | bytes 41877504 | tf_op jit(solution)/shard_map/reshape | solution.py:26
  260.6 19.6 %fusion = f32[512,3,512]{2,0,1:T(8,128)S(1)} fusion(bf16[8192,3,512]{0,2,1:T(8,128)(2,1)} %copy.10, bf16[512,8192]{1,0:T(8,128)(2,1)} %all-gather.3.cloned.1.call-done), kind=kOutput, calls=%fused_computation | convolution fusion | flops 12884901888 | bytes 36700160 | tf_op jit(solution)/shard_map/dot_general | solution.py:39
  282.1 2.1 copy.11
  284.2 9.2 %fusion.2 = f32[32,16,512]{2,1,0:T(8,128)} fusion(bf16[512,32,16]{0,2,1:T(8,128)(2,1)} %bitcast.72, bf16[32,512,639]{2,1,0:T(8,128)(2,1)} %reshape.30), kind=kOutput, calls=%fused_computation.2 | convolution fusion | flops 268435456 | bytes 18350080 | tf_op jit(solution)/shard_map/fst,sfg->tfg/dot_general | solution.py:52
  293.4 2.6 copy.12
  296.0 2.5 fusion.14
  298.6 78.9 %all-gather.5.cloned.1.call-done = bf16[512,8192]{1,0:T(8,128)(2,1)} async-done(((bf16[512,512]{1,0:T(8,128)(2,1)}), bf16[512,8192]{1,0:T(8,128)(2,1)}) %all-gather.5.cloned.1.call-update) | async-done | bytes 8388624 | tf_op jit(solution)/shard_map/all_gather | solution.py:58
  377.5 11.1 %fusion.9 = bf16[512,512]{1,0:T(8,128)(2,1)} fusion(bf16[512,8192]{1,0:T(8,128)(2,1)} %all-gather.5.cloned.1.call-done, bf16[8192,512]{1,0:T(8,128)(2,1)} %bitcast.30, bf16[512,512]{1,0:T(8,128)(2,1)} %param.7), kind=kOutput, calls=%fused_computation.14 | convolution fusion | flops 4295753728 | bytes 17825792 | tf_op jit(solution)/shard_map/dot_general | solution.py:57
  (25 shorter events, 16.3 us)
Async XLA Ops:
  6.5 254.1 %all-gather.3.cloned.1.call-start = ((), (), s32[]{:S(2)}) async-start(), calls=%async_computation.1 | async-start | bytes 8912896 | tf_op jit(solution)/shard_map/all_gather | solution.py:40
  74.9 223.6 %all-to-all-start = ((bf16[16,512,512]{2,1,0:T(8,128)(2,1)}), bf16[16,512,512]{2,1,0:T(8,128)(2,1)}, u32[]{:S(2)}, u32[]{:S(2)}) async-start(bf16[16,512,512]{2,1,0:T(8,128)(2,1)} %bitcast_dynamic-update-slice_fusion), calls=%async_computation | async-start | bytes 16777216 | tf_op jit(solution)/shard_map/all_to_all | solution.py:11
  79.8 33.6 %copy-start.1 = (bf16[32,128]{1,0:T(8,128)(2,1)S(1)}, bf16[32,128]{1,0:T(8,128)(2,1)}, u32[]{:S(2)}) copy-start(bf16[32,128]{1,0:T(8,128)(2,1)} %param.11) | copy-start | bytes 24580
  79.8 297.6 %all-gather.5.cloned.1.call-start = ((), (), s32[]{:S(2)}) async-start(), calls=%async_computation.2 | async-start | bytes 8912896 | tf_op jit(solution)/shard_map/all_gather | solution.py:58
  191.6 69.0 %copy-start = (f32[3,3,512]{2,1,0:T(4,128)S(1)}, f32[3,3,512]{2,1,0:T(4,128)}, u32[]{:S(2)}) copy-start(f32[3,3,512]{2,1,0:T(4,128)} %param.10) | copy-start | bytes 55300
  284.2 11.8 %copy-start.2 = (f32[512]{0:T(512)S(1)}, f32[512]{0:T(512)}, u32[]{:S(2)}) copy-start(f32[512]{0:T(512)} %param.12) | copy-start | bytes 6148
Sparse Core Ops, SparseCore 0:
  44.9 133.4 all-gather.2
  298.7 78.7 all-gather.4
